TPU v7x, 32 devices: a whole 2x2x4 slice. The times are simulated.
32 devices in a mesh: section: 2 (over x), wrow: 4 (over y, core), wcol: 4 (over z).
Axes of the slice: x: 2, y: 2, z: 4, core: 2. Of those that a mesh axis runs over, the one named last changes fastest.
Arguments:
- states: bfloat16 [2, 64, 64, 1536], P(None, 'wrow', 'wcol'), may hold values from -6 to 6
- timesteps: int32 [2], replicated, may hold values from 0 to 999, as said below
- shifts: int32 [2, 2], P('section'), may hold values from 1 to 4
- qkv_weight: bfloat16 [2, 1536, 2304], P('section', None, 'wcol'), may hold values from -0.15625 to 0.15625
- out_weight: bfloat16 [2, 768, 1536], P('section', None, 'wcol'), may hold values from -0.21875 to 0.21875
- mod_weight: bfloat16 [2, 256, 4608], P('section', None, 'wcol'), may hold values from -0.375 to 0.375
Outputs:
- layer_states: bfloat16 [2, 2, 64, 64, 1536], P('section', None, 'wrow', 'wcol')
Inputs may be any that keep to these rules, and one draw needn't show every extreme that they name: The 2 timesteps are distinct.
All inputs are finite; a program needn't handle non-finite values.
Results may differ from a plain program's by a relative error of at most 0.0053.
Values may be sent and summed in bfloat16 or wider, within the bound.
No kernel may reach another device: no remote copies, remote signals or barrier semaphores. Data moves between devices by JAX's collectives and lax.ppermute only.
A program may use at most 128 MiB of HBM per device.

v0:
```python
import math
import jax
import jax.numpy as jnp
from jax import lax
from jax.sharding import PartitionSpec as P

HEADS = 6
HD = 128
TEMB = 256
WIN = 8
MB = 2
epsilon = 1e-06


def passed_along(shard, axis, by):
    devices = lax.axis_size(axis)
    return lax.ppermute(shard, axis, [(i, (i + by) % devices) for i in range(devices)])


def from_behind(shard, axis, by):
    devices = lax.axis_size(axis)
    pairs = [(i, i + by) for i in range(devices) if 0 <= i + by < devices]
    return lax.ppermute(shard, axis, pairs)


def sinusoid(moments, entries):
    half_count = entries // 2
    frequency = jnp.exp(-math.log(10000.0) * jnp.arange(half_count, dtype=jnp.float32) / half_count)
    angles = moments.astype(jnp.float32)[:, None] * frequency[None, :]
    return jnp.concatenate([jnp.cos(angles), jnp.sin(angles)], axis=1)


def layer_norm(region):
    values = region.astype(jnp.float32)
    center = values - jnp.mean(values, axis=-1, keepdims=True)
    spread = jnp.mean(center * center, axis=-1, keepdims=True)
    return center * lax.rsqrt(spread + epsilon)


def window_attention(triples):
    tile_rows, tile_cols, feature_width = triples.shape
    windowed = triples.reshape(tile_rows // WIN, WIN, tile_cols // WIN, WIN, 3, HEADS, HD)
    windowed = windowed.transpose(4, 0, 2, 5, 1, 3, 6).reshape(
        3, tile_rows // WIN * (tile_cols // WIN), HEADS, WIN * WIN, HD
    )
    scores = jnp.einsum(
        "nhqd,nhkd->nhqk", windowed[0], windowed[1], preferred_element_type=jnp.float32
    ) * HD ** (-0.5)
    weights = jnp.exp(scores)
    probabilities = (weights / jnp.sum(weights, axis=-1, keepdims=True)).astype(jnp.bfloat16)
    attended = jnp.einsum(
        "nhqk,nhkd->nhqd", probabilities, windowed[2], preferred_element_type=jnp.float32
    ).astype(jnp.bfloat16)
    attended = attended.reshape(tile_rows // WIN, tile_cols // WIN, HEADS, WIN, WIN, HD).transpose(
        0, 3, 1, 4, 2, 5
    )
    return attended.reshape(tile_rows, tile_cols, HEADS * HD)


def project(region, matrix):
    tile_rows, tile_cols, feature_width = region.shape
    product = jnp.dot(
        region.reshape(tile_rows * tile_cols, feature_width),
        matrix,
        preferred_element_type=jnp.float32,
    )
    return product.reshape(tile_rows, tile_cols, -1)


def splice(region, border, amount, direction, margin, axis_index):
    if direction > 0:
        longer = jnp.concatenate([region, border], axis=axis_index)
        offset = amount
    else:
        longer = jnp.concatenate([border, region], axis=axis_index)
        offset = margin - amount
    return lax.dynamic_slice_in_dim(longer, offset, region.shape[axis_index], axis_index)


def wrap_rim(region, row_shift, col_shift, direction):
    margin = WIN // 2
    if direction > 0:
        border = region[:margin]
    else:
        border = region[region.shape[0] - margin :]
    border = passed_along(border, "wrow", -direction)
    region = splice(region, border, row_shift, direction, margin, 0)
    if direction > 0:
        border = region[:, :margin]
    else:
        border = region[:, region.shape[1] - margin :]
    border = passed_along(border, "wcol", -direction)
    return splice(region, border, col_shift, direction, margin, 1)


def shifted_layer(inputs, modulation, row_shift, col_shift, qkv_matrix, out_matrix):
    feature_width = inputs.shape[-1]
    mod_shift = modulation[:feature_width]
    mod_scale = modulation[feature_width : 2 * feature_width]
    mod_gate = modulation[2 * feature_width :]
    normed = (layer_norm(inputs) * (1.0 + mod_scale) + mod_shift).astype(jnp.bfloat16)
    rolled = wrap_rim(normed, row_shift, col_shift, 1)
    triples = project(rolled, qkv_matrix).astype(jnp.bfloat16)
    attended = window_attention(triples)
    projection = project(attended, out_matrix).astype(jnp.bfloat16)
    projection = wrap_rim(projection, row_shift, col_shift, -1).astype(jnp.float32)
    return (inputs.astype(jnp.float32) + mod_gate * projection).astype(jnp.bfloat16)


def slice_part(matrix, position, across):
    piece_width = matrix.shape[1] // across
    return lax.dynamic_slice_in_dim(matrix, position * piece_width, piece_width, 1)


def regroup(matrix, across, along):
    leading = matrix.shape[0]
    piece_width = matrix.shape[1] // (across * along)
    return (
        matrix.reshape(leading, across, along, piece_width)
        .transpose(0, 2, 1, 3)
        .reshape(leading, -1)
    )


def per_device(states, timesteps, shifts, qkv_weight, out_weight, mod_weight):
    embedding = jax.nn.silu(sinusoid(timesteps, TEMB)).astype(jnp.bfloat16)
    mod_part = jnp.dot(embedding, mod_weight[0], preferred_element_type=jnp.float32).astype(
        jnp.bfloat16
    )
    across = lax.axis_size("wrow")
    along = lax.axis_size("wcol")
    position = lax.axis_index("wrow")
    gathered = (
        lax.all_gather(
            slice_part(qkv_weight[0], position, across), ("wrow", "wcol"), axis=1, tiled=True
        ),
        lax.all_gather(
            slice_part(out_weight[0], position, across), ("wrow", "wcol"), axis=1, tiled=True
        ),
        lax.all_gather(
            slice_part(mod_part, position, across), ("wrow", "wcol"), axis=1, tiled=True
        ),
    )
    qkv_full = regroup(gathered[0], across, along)
    out_full = regroup(gathered[1], across, along)
    modulations = regroup(gathered[2], across, along)
    section_index = lax.axis_index("section")
    moments = MB + lax.axis_size("section") - 1
    row_shift = shifts[0, 0]
    col_shift = shifts[0, 1]
    incoming = jnp.zeros_like(states[0])
    results = jnp.zeros_like(states)
    for moment in range(moments):
        member = moment - section_index
        batch_slot = jnp.clip(member, 0, MB - 1)
        block_input = jnp.where(section_index == 0, states[min(moment, MB - 1)], incoming)
        modulation = lax.dynamic_index_in_dim(modulations, batch_slot, 0, keepdims=False).astype(
            jnp.float32
        )
        outgoing = shifted_layer(block_input, modulation, row_shift, col_shift, qkv_full, out_full)
        active = (member >= 0) & (member < MB)
        updated = lax.dynamic_update_index_in_dim(results, outgoing, batch_slot, 0)
        results = jnp.where(active, updated, results)
        if moment + 1 < moments:
            incoming = from_behind(outgoing, "section", 1)
    return results[None]


def solution(mesh):
    in_specs = (
        P(None, "wrow", "wcol", None),
        P(),
        P("section", None),
        P("section", None, "wcol"),
        P("section", None, "wcol"),
        P("section", None, "wcol"),
    )
    out_specs = P("section", None, "wrow", "wcol", None)
    return jax.shard_map(
        per_device, mesh=mesh, in_specs=in_specs, out_specs=out_specs, check_vma=False
    )
```

profile of v0, /device:TPU:0, one launch (start us, length us, event | category | flops | bytes accessed | tf_op | source)
XLA Modules:
  0.0 278.9 jit_solution(11938716838353509522)
XLA Ops:
  6.5 1.3 constant_dynamic-slice_fusion
  7.8 0.8 copy.116
  8.7 0.8 constant_dynamic-slice_fusion.1
  9.7 1.3 fusion.46
  11.0 34.5 %all-gather.2 = bf16[16,288,2]{1,2,0:T(2,128)(2,1)S(1)} all-gather(bf16[1,288,2]{1,2,0:T(2,128)(2,1)S(1)} %fusion.62), channel_id=1, replica_groups=mesh['section'=2,'wrow'=4,'wcol'=4] {'wrow','wcol'}, dimensions={0}, use_global_device_ids=true | all-gather | bytes 19584 | tf_op jit(solution)/shard_map/all_gather | solution.py:140
  47.6 0.9 copy-done.9
  51.7 1.3 fusion.31
  55.1 3.3 %copy.85 = bf16[768,4,4,96]{0,3,2,1:T(8,128)(2,1)} copy(bf16[768,4,4,96]{0,3,1,2:T(8,128)(2,1)} %bitcast.135) | data formatting | bytes 4718592 | tf_op jit(solution)/shard_map/transpose | solution.py:120
  58.3 63.5 %all-gather.6.cloned.1.call-done = bf16[1,1536,2304]{1,2,0:T(8,128)(2,1)} async-done(((bf16[1,1536,144]{1,2,0:T(8,128)(2,1)}), bf16[1,1536,2304]{1,2,0:T(8,128)(2,1)}) %all-gather.6.cloned.1.call-update) | async-done | bytes 7077904 | tf_op jit(solution)/shard_map/all_gather | solution.py:134
  121.8 3.6 %copy.77 = bf16[1536,4,4,144]{0,3,2,1:T(8,128)(2,1)S(1)} copy(bf16[1536,4,4,144]{0,3,1,2:T(8,128)(2,1)} %bitcast.131) | data formatting | bytes 14155776 | tf_op jit(solution)/shard_map/transpose | solution.py:120
  125.4 2.4 convolution_convert_fusion.2
  129.5 2.5 convolution_convert_fusion.5
  133.6 3.6 %collective-permute-done.2 = bf16[4,16,1536]{2,1,0:T(8,128)(2,1)S(1)} collective-permute-done((bf16[4,16,1536]{2,1,0:T(8,128)(2,1)S(1)}, bf16[4,16,1536]{2,1,0:T(8,128)(2,1)S(1)}, u32[]{:S(2)}, u32[]{:S(2)}) %collective-permute-start.2) | collective-permute-done | bytes 196640 | tf_op jit(solution)/shard_map/ppermute | solution.py:17
  137.3 0.9 copy-done.10
  138.3 1.6 collective-permute-start.3
  141.2 4.6 %collective-permute-done.3 = bf16[16,4,1536]{2,1,0:T(4,128)(2,1)S(1)} collective-permute-done((bf16[16,4,1536]{2,1,0:T(4,128)(2,1)S(1)}, bf16[16,4,1536]{2,1,0:T(4,128)(2,1)S(1)}, u32[]{:S(2)}, u32[]{:S(2)}) %collective-permute-start.3) | collective-permute-done | bytes 196640 | tf_op jit(solution)/shard_map/ppermute | solution.py:17
  146.0 2.0 bitcast_dynamic-update-slice_fusion
  148.1 3.4 %collective-permute-start.4 = (bf16[16,16,1536]{2,1,0:T(8,128)(2,1)S(1)}, bf16[16,16,1536]{2,1,0:T(8,128)(2,1)S(1)}, u32[]{:S(2)}, u32[]{:S(2)}) collective-permute-start(bf16[16,16,1536]{2,1,0:T(8,128)(2,1)S(1)} %get-tuple-element.21), channel_id=1, source_target_pairs={{0,16},{1,17},{2,18},{3,19},{4,20},{5,21},{6,22},{7,23},{8,24},{9,... | collective-permute-start | bytes 2359304 | tf_op jit(solution)/shard_map/ppermute | solution.py:23
  151.5 13.9 %collective-permute-done.4 = bf16[16,16,1536]{2,1,0:T(8,128)(2,1)S(1)} collective-permute-done((bf16[16,16,1536]{2,1,0:T(8,128)(2,1)S(1)}, bf16[16,16,1536]{2,1,0:T(8,128)(2,1)S(1)}, u32[]{:S(2)}, u32[]{:S(2)}) %collective-permute-start.4) | collective-permute-done | bytes 786464 | tf_op jit(solution)/shard_map/ppermute | solution.py:23
  166.6 3.2 %collective-permute-done.5 = bf16[4,16,1536]{2,1,0:T(8,128)(2,1)S(1)} collective-permute-done((bf16[4,16,1536]{2,1,0:T(8,128)(2,1)S(1)}, bf16[4,16,1536]{2,1,0:T(8,128)(2,1)S(1)}, u32[]{:S(2)}, u32[]{:S(2)}) %collective-permute-start.5) | collective-permute-done | bytes 196640 | tf_op jit(solution)/shard_map/ppermute | solution.py:17
  170.6 6.1 %collective-permute-done.6 = bf16[16,4,1536]{2,1,0:T(4,128)(2,1)S(1)} collective-permute-done((bf16[16,4,1536]{2,1,0:T(4,128)(2,1)S(1)}, bf16[16,4,1536]{2,1,0:T(4,128)(2,1)S(1)}, u32[]{:S(2)}, u32[]{:S(2)}) %collective-permute-start.6) | collective-permute-done | bytes 196640 | tf_op jit(solution)/shard_map/ppermute | solution.py:17
  176.7 5.4 %convolution_convert_fusion.1 = bf16[16,16,2304]{2,1,0:T(8,128)(2,1)S(1)} fusion(bf16[1536,2304,1]{0,1,2:T(8,128)(2,1)} %bitcast.129, s32[]{:T(128)S(6)} %select_n.93, bf16[16,16,1536]{2,1,0:T(8,128)(2,1)S(1)} %fusion.29, bf16[16,4,1536]{2,1,0:T(4,128)(2,1)S(1)} %collective-permute-done.6), kind=kOutput, calls=%fused_computation.1 | convolution fusion | flops 1814102016 | bytes 9240580 | tf_op jit(solution)/shard_map/dot_general | solution.py:62
  182.4 0.8 copy.90
  183.2 1.2 fusion.24
  184.5 2.6 convolution_convert_fusion.7
  187.1 1.1 copy.92
  188.1 2.5 convolution_convert_fusion.4
  190.6 1.2 collective-permute-start.7
  191.8 3.9 %collective-permute-done.7 = bf16[4,16,1536]{2,1,0:T(8,128)(2,1)S(1)} collective-permute-done((bf16[4,16,1536]{2,1,0:T(8,128)(2,1)S(1)}, bf16[4,16,1536]{2,1,0:T(8,128)(2,1)S(1)}, u32[]{:S(2)}, u32[]{:S(2)}) %collective-permute-start.7) | collective-permute-done | bytes 196640 | tf_op jit(solution)/shard_map/ppermute | solution.py:17
  195.9 0.9 copy-done.8
  196.8 0.8 slice.192
  197.6 9.1 %collective-permute-done.8 = bf16[16,4,1536]{2,1,0:T(4,128)(2,1)S(1)} collective-permute-done((bf16[16,4,1536]{2,1,0:T(4,128)(2,1)}, bf16[16,4,1536]{2,1,0:T(4,128)(2,1)S(1)}, u32[]{:S(2)}, u32[]{:S(2)}) %collective-permute-start.8) | collective-permute-done | bytes 196640 | tf_op jit(solution)/shard_map/ppermute | solution.py:17
  206.7 2.3 fusion.45
  209.0 4.4 %collective-permute-start.9 = (bf16[16,16,1536]{2,1,0:T(8,128)(2,1)S(1)}, bf16[16,16,1536]{2,1,0:T(8,128)(2,1)S(1)}, u32[]{:S(2)}, u32[]{:S(2)}) collective-permute-start(bf16[16,16,1536]{2,1,0:T(8,128)(2,1)S(1)} %get-tuple-element.17), channel_id=1, source_target_pairs={{0,16},{1,17},{2,18},{3,19},{4,20},{5,21},{6,22},{7,23},{8,24},{9,... | collective-permute-start | bytes 2359304 | tf_op jit(solution)/shard_map/ppermute | solution.py:23
  213.5 16.3 %collective-permute-done.9 = bf16[16,16,1536]{2,1,0:T(8,128)(2,1)S(1)} collective-permute-done((bf16[16,16,1536]{2,1,0:T(8,128)(2,1)S(1)}, bf16[16,16,1536]{2,1,0:T(8,128)(2,1)S(1)}, u32[]{:S(2)}, u32[]{:S(2)}) %collective-permute-start.9) | collective-permute-done | bytes 786464 | tf_op jit(solution)/shard_map/ppermute | solution.py:23
  231.0 3.2 %collective-permute-done.10 = bf16[4,16,1536]{2,1,0:T(8,128)(2,1)S(1)} collective-permute-done((bf16[4,16,1536]{2,1,0:T(8,128)(2,1)S(1)}, bf16[4,16,1536]{2,1,0:T(8,128)(2,1)S(1)}, u32[]{:S(2)}, u32[]{:S(2)}) %collective-permute-start.10) | collective-permute-done | bytes 196640 | tf_op jit(solution)/shard_map/ppermute | solution.py:17
  234.8 7.0 %collective-permute-done.11 = bf16[16,4,1536]{2,1,0:T(4,128)(2,1)S(1)} collective-permute-done((bf16[16,4,1536]{2,1,0:T(4,128)(2,1)S(1)}, bf16[16,4,1536]{2,1,0:T(4,128)(2,1)S(1)}, u32[]{:S(2)}, u32[]{:S(2)}) %collective-permute-start.11) | collective-permute-done | bytes 196640 | tf_op jit(solution)/shard_map/ppermute | solution.py:17
  241.8 5.4 %convolution_convert_fusion = bf16[16,16,2304]{2,1,0:T(8,128)(2,1)S(1)} fusion(bf16[1536,2304,1]{0,1,2:T(8,128)(2,1)} %bitcast.130, s32[]{:T(128)S(6)} %select_n.93, bf16[16,16,1536]{2,1,0:T(8,128)(2,1)S(1)} %fusion.27, bf16[16,4,1536]{2,1,0:T(4,128)(2,1)S(1)} %collective-permute-done.11), kind=kOutput, calls=%fused_computation | convolution fusion | flops 1814102016 | bytes 9240580 | tf_op jit(solution)/shard_map/dot_general | solution.py:62
  247.5 0.8 copy.97
  248.3 1.2 fusion.23
  249.5 2.6 convolution_convert_fusion.6
  252.1 1.1 copy.99
  253.2 2.5 convolution_convert_fusion.3
  255.8 5.1 %collective-permute-done.12 = bf16[4,16,1536]{2,1,0:T(8,128)(2,1)S(1)} collective-permute-done((bf16[4,16,1536]{2,1,0:T(8,128)(2,1)S(1)}, bf16[4,16,1536]{2,1,0:T(8,128)(2,1)S(1)}, u32[]{:S(2)}, u32[]{:S(2)}) %collective-permute-start.12) | collective-permute-done | bytes 196640 | tf_op jit(solution)/shard_map/ppermute | solution.py:17
  261.0 0.9 copy-done.12
  262.1 1.1 copy.121
  263.2 6.4 %collective-permute-done.13 = bf16[16,4,1536]{2,1,0:T(4,128)(2,1)} collective-permute-done((bf16[16,4,1536]{2,1,0:T(4,128)(2,1)S(1)}, bf16[16,4,1536]{2,1,0:T(4,128)(2,1)}, u32[]{:S(2)}, u32[]{:S(2)}) %collective-permute-start.13) | collective-permute-done | bytes 196640 | tf_op jit(solution)/shard_map/ppermute | solution.py:17
  269.6 2.5 fusion.44
  (108 shorter events, 11.0 us)
Async XLA Ops:
  6.5 2.2 copy-start
  6.5 3.0 %copy-start.17 = (s32[2]{0:T(128)S(1)}, s32[2]{0:T(128)}, u32[]{:S(2)}) copy-start(s32[2]{0:T(128)} %param.7) | copy-start | bytes 28
  6.5 48.5 %all-gather.8.cloned.1.call-start = ((), (), s32[]{:S(2)}) async-start(), calls=%async_computation.1 | async-start | bytes 2506752 | tf_op jit(solution)/shard_map/all_gather | solution.py:137
  6.5 40.0 %copy-start.1 = (bf16[2,16,16,1536]{3,2,1,0:T(8,128)(2,1)S(1)}, bf16[2,16,16,1536]{3,2,1,0:T(8,128)(2,1)}, u32[]{:S(2)}) copy-start(bf16[2,16,16,1536]{3,2,1,0:T(8,128)(2,1)} %param.6) | copy-start | bytes 4718596
  8.7 113.2 %all-gather.6.cloned.1.call-start = ((), (), s32[]{:S(2)}) async-start(), calls=%async_computation | async-start | bytes 7520256 | tf_op jit(solution)/shard_map/all_gather | solution.py:134
  46.8 1.7 copy-start.16
  47.6 0.9 copy-start.9
  48.5 3.2 %collective-permute-start = (bf16[4,16,1536]{2,1,0:T(8,128)(2,1)S(1)}, bf16[4,16,1536]{2,1,0:T(8,128)(2,1)S(1)}, u32[]{:S(2)}, u32[]{:S(2)}) collective-permute-start(bf16[4,16,1536]{2,1,0:T(8,128)(2,1)S(1)} %slice.176), channel_id=1, source_target_pairs={{0,12},{4,0},{8,4},{12,8},{1,13},{5,1},{9,5},{13,9},{2,14},{6,2},{... | collective-permute-start | bytes 589832 | tf_op jit(solution)/shard_map/ppermute | solution.py:17
  53.1 72.4 %collective-permute-start.1 = (bf16[16,4,1536]{2,1,0:T(4,128)(2,1)S(1)}, bf16[16,4,1536]{2,1,0:T(4,128)(2,1)S(1)}, u32[]{:S(2)}, u32[]{:S(2)}) collective-permute-start(bf16[16,4,1536]{2,1,0:T(4,128)(2,1)S(1)} %slice.177), channel_id=1, source_target_pairs={{0,3},{1,0},{2,1},{3,2},{4,7},{5,4},{6,5},{7,6},{8,11},{9,8},{10,9... | collective-permute-start | bytes 589832 | tf_op jit(solution)/shard_map/ppermute | solution.py:17
  125.4 2.9 %copy-start.7 = (bf16[1536,4,4,144]{0,3,2,1:T(8,128)(2,1)}, bf16[1536,4,4,144]{0,3,2,1:T(8,128)(2,1)S(1)}, u32[]{:S(2)}) copy-start(bf16[1536,4,4,144]{0,3,2,1:T(8,128)(2,1)S(1)} %copy.77) | copy-start | bytes 21233668
  132.0 5.1 %collective-permute-start.2 = (bf16[4,16,1536]{2,1,0:T(8,128)(2,1)S(1)}, bf16[4,16,1536]{2,1,0:T(8,128)(2,1)S(1)}, u32[]{:S(2)}, u32[]{:S(2)}) collective-permute-start(bf16[4,16,1536]{2,1,0:T(8,128)(2,1)S(1)} %slice.181), channel_id=1, source_target_pairs={{0,4},{4,8},{8,12},{12,0},{1,5},{5,9},{9,13},{13,1},{2,6},{6,10},{... | collective-permute-start | bytes 589832 | tf_op jit(solution)/shard_map/ppermute | solution.py:17
  137.3 0.9 copy-start.10
  138.3 7.5 %collective-permute-start.3 = (bf16[16,4,1536]{2,1,0:T(4,128)(2,1)S(1)}, bf16[16,4,1536]{2,1,0:T(4,128)(2,1)S(1)}, u32[]{:S(2)}, u32[]{:S(2)}) collective-permute-start(bf16[16,4,1536]{2,1,0:T(4,128)(2,1)S(1)} %slice.182), channel_id=1, source_target_pairs={{0,1},{1,2},{2,3},{3,0},{4,5},{5,6},{6,7},{7,4},{8,9},{9,10},{10,1... | collective-permute-start | bytes 589832 | tf_op jit(solution)/shard_map/ppermute | solution.py:17
  141.2 4.8 %copy-start.11 = (bf16[16,16,1536]{2,1,0:T(8,128)(2,1)S(1)}, bf16[16,16,1536]{2,1,0:T(8,128)(2,1)}, u32[]{:S(2)}) copy-start(bf16[16,16,1536]{2,1,0:T(8,128)(2,1)} %copy-done.10) | copy-start | bytes 2359300
  146.0 5.5 %copy-start.15 = (f32[1,4608]{1,0:T(1,128)S(1)}, f32[1,4608]{1,0:T(1,128)}, u32[]{:S(2)}) copy-start(f32[1,4608]{1,0:T(1,128)} %get-tuple-element.32) | copy-start | bytes 55300
  146.0 19.4 %copy-start.2 = (bf16[2,16,16,1536]{3,2,1,0:T(8,128)(2,1)S(1)}, bf16[2,16,16,1536]{3,2,1,0:T(8,128)(2,1)}, u32[]{:S(2)}) copy-start(bf16[2,16,16,1536]{3,2,1,0:T(8,128)(2,1)} %param.6) | copy-start | bytes 4718596
  148.1 17.4 %collective-permute-start.4 = (bf16[16,16,1536]{2,1,0:T(8,128)(2,1)S(1)}, bf16[16,16,1536]{2,1,0:T(8,128)(2,1)S(1)}, u32[]{:S(2)}, u32[]{:S(2)}) collective-permute-start(bf16[16,16,1536]{2,1,0:T(8,128)(2,1)S(1)} %get-tuple-element.21), channel_id=1, source_target_pairs={{0,16},{1,17},{2,18},{3,19},{4,20},{5,21},{6,22},{7,23},{8,24},{9,... | collective-permute-start | bytes 2359304 | tf_op jit(solution)/shard_map/ppermute | solution.py:23
  165.7 4.2 %copy-start.4 = (bf16[16,16,1536]{2,1,0:T(8,128)(2,1)}, bf16[16,16,1536]{2,1,0:T(8,128)(2,1)S(1)}, u32[]{:S(2)}) copy-start(bf16[16,16,1536]{2,1,0:T(8,128)(2,1)S(1)} %get-tuple-element.19) | copy-start | bytes 2359300
  166.5 3.2 %collective-permute-start.5 = (bf16[4,16,1536]{2,1,0:T(8,128)(2,1)S(1)}, bf16[4,16,1536]{2,1,0:T(8,128)(2,1)S(1)}, u32[]{:S(2)}, u32[]{:S(2)}) collective-permute-start(bf16[4,16,1536]{2,1,0:T(8,128)(2,1)S(1)} %slice.186), channel_id=1, source_target_pairs={{0,12},{4,0},{8,4},{12,8},{1,13},{5,1},{9,5},{13,9},{2,14},{6,2},{... | collective-permute-start | bytes 589832 | tf_op jit(solution)/shard_map/ppermute | solution.py:17
  170.0 6.7 %collective-permute-start.6 = (bf16[16,4,1536]{2,1,0:T(4,128)(2,1)S(1)}, bf16[16,4,1536]{2,1,0:T(4,128)(2,1)S(1)}, u32[]{:S(2)}, u32[]{:S(2)}) collective-permute-start(bf16[16,4,1536]{2,1,0:T(4,128)(2,1)S(1)} %slice.187), channel_id=1, source_target_pairs={{0,3},{1,0},{2,1},{3,2},{4,7},{5,4},{6,5},{7,6},{8,11},{9,8},{10,9... | collective-permute-start | bytes 589832 | tf_op jit(solution)/shard_map/ppermute | solution.py:17
  190.6 5.1 %collective-permute-start.7 = (bf16[4,16,1536]{2,1,0:T(8,128)(2,1)S(1)}, bf16[4,16,1536]{2,1,0:T(8,128)(2,1)S(1)}, u32[]{:S(2)}, u32[]{:S(2)}) collective-permute-start(bf16[4,16,1536]{2,1,0:T(8,128)(2,1)S(1)} %slice.191), channel_id=1, source_target_pairs={{0,4},{4,8},{8,12},{12,0},{1,5},{5,9},{9,13},{13,1},{2,6},{6,10},{... | collective-permute-start | bytes 589832 | tf_op jit(solution)/shard_map/ppermute | solution.py:17
  195.9 0.9 copy-start.8
  197.6 9.1 %collective-permute-start.8 = (bf16[16,4,1536]{2,1,0:T(4,128)(2,1)}, bf16[16,4,1536]{2,1,0:T(4,128)(2,1)S(1)}, u32[]{:S(2)}, u32[]{:S(2)}) collective-permute-start(bf16[16,4,1536]{2,1,0:T(4,128)(2,1)} %slice.192), channel_id=1, source_target_pairs={{0,1},{1,2},{2,3},{3,0},{4,5},{5,6},{6,7},{7,4},{8,9},{9,10},{10,1... | collective-permute-start | bytes 589832 | tf_op jit(solution)/shard_map/ppermute | solution.py:17
  206.7 6.8 %copy-start.14 = (f32[1,4608]{1,0:T(1,128)S(1)}, f32[1,4608]{1,0:T(1,128)}, u32[]{:S(2)}) copy-start(f32[1,4608]{1,0:T(1,128)} %get-tuple-element.31) | copy-start | bytes 55300
  206.7 23.1 %copy-start.3 = (bf16[2,16,16,1536]{3,2,1,0:T(8,128)(2,1)S(1)}, bf16[2,16,16,1536]{3,2,1,0:T(8,128)(2,1)}, u32[]{:S(2)}) copy-start(bf16[2,16,16,1536]{3,2,1,0:T(8,128)(2,1)} %param.6) | copy-start | bytes 4718596
  209.0 20.8 %collective-permute-start.9 = (bf16[16,16,1536]{2,1,0:T(8,128)(2,1)S(1)}, bf16[16,16,1536]{2,1,0:T(8,128)(2,1)S(1)}, u32[]{:S(2)}, u32[]{:S(2)}) collective-permute-start(bf16[16,16,1536]{2,1,0:T(8,128)(2,1)S(1)} %get-tuple-element.17), channel_id=1, source_target_pairs={{0,16},{1,17},{2,18},{3,19},{4,20},{5,21},{6,22},{7,23},{8,24},{9,... | collective-permute-start | bytes 2359304 | tf_op jit(solution)/shard_map/ppermute | solution.py:23
  230.1 4.3 %copy-start.5 = (bf16[16,16,1536]{2,1,0:T(8,128)(2,1)}, bf16[16,16,1536]{2,1,0:T(8,128)(2,1)S(1)}, u32[]{:S(2)}) copy-start(bf16[16,16,1536]{2,1,0:T(8,128)(2,1)S(1)} %get-tuple-element.15) | copy-start | bytes 2359300
  230.9 3.2 %collective-permute-start.10 = (bf16[4,16,1536]{2,1,0:T(8,128)(2,1)S(1)}, bf16[4,16,1536]{2,1,0:T(8,128)(2,1)S(1)}, u32[]{:S(2)}, u32[]{:S(2)}) collective-permute-start(bf16[4,16,1536]{2,1,0:T(8,128)(2,1)S(1)} %slice.196), channel_id=1, source_target_pairs={{0,12},{4,0},{8,4},{12,8},{1,13},{5,1},{9,5},{13,9},{2,14},{6,2},{... | collective-permute-start | bytes 589832 | tf_op jit(solution)/shard_map/ppermute | solution.py:17
  234.4 7.3 %collective-permute-start.11 = (bf16[16,4,1536]{2,1,0:T(4,128)(2,1)S(1)}, bf16[16,4,1536]{2,1,0:T(4,128)(2,1)S(1)}, u32[]{:S(2)}, u32[]{:S(2)}) collective-permute-start(bf16[16,4,1536]{2,1,0:T(4,128)(2,1)S(1)} %slice.197), channel_id=1, source_target_pairs={{0,3},{1,0},{2,1},{3,2},{4,7},{5,4},{6,5},{7,6},{8,11},{9,8},{10,9... | collective-permute-start | bytes 589832 | tf_op jit(solution)/shard_map/ppermute | solution.py:17
  255.7 5.1 %collective-permute-start.12 = (bf16[4,16,1536]{2,1,0:T(8,128)(2,1)S(1)}, bf16[4,16,1536]{2,1,0:T(8,128)(2,1)S(1)}, u32[]{:S(2)}, u32[]{:S(2)}) collective-permute-start(bf16[4,16,1536]{2,1,0:T(8,128)(2,1)S(1)} %slice.201), channel_id=1, source_target_pairs={{0,4},{4,8},{8,12},{12,0},{1,5},{5,9},{9,13},{13,1},{2,6},{6,10},{... | collective-permute-start | bytes 589832 | tf_op jit(solution)/shard_map/ppermute | solution.py:17
  261.0 0.9 copy-start.12
  262.0 7.6 %collective-permute-start.13 = (bf16[16,4,1536]{2,1,0:T(4,128)(2,1)S(1)}, bf16[16,4,1536]{2,1,0:T(4,128)(2,1)}, u32[]{:S(2)}, u32[]{:S(2)}) collective-permute-start(bf16[16,4,1536]{2,1,0:T(4,128)(2,1)S(1)} %slice.202), channel_id=1, source_target_pairs={{0,1},{1,2},{2,3},{3,0},{4,5},{5,6},{6,7},{7,4},{8,9},{9,10},{10,1... | collective-permute-start | bytes 589832 | tf_op jit(solution)/shard_map/ppermute | solution.py:17
  262.0 7.6 %copy-start.6 = (bf16[16,16,1536]{2,1,0:T(8,128)(2,1)S(1)}, bf16[16,16,1536]{2,1,0:T(8,128)(2,1)}, u32[]{:S(2)}) copy-start(bf16[16,16,1536]{2,1,0:T(8,128)(2,1)} %copy-done.5) | copy-start | bytes 2359300
  262.0 7.5 %copy-start.13 = (bf16[16,16,1536]{2,1,0:T(8,128)(2,1)S(1)}, bf16[16,16,1536]{2,1,0:T(8,128)(2,1)}, u32[]{:S(2)}) copy-start(bf16[16,16,1536]{2,1,0:T(8,128)(2,1)} %copy-done.12) | copy-start | bytes 2359300
Sparse Core Ops, SparseCore 0:
  9.6 45.0 all-gather.7
  57.0 64.7 all-gather.5
where the time goes:
time: 280 us; the launch traced here: 279 us
  waiting for transfers between devices  147 us (52%)
  blocking collectives  34.5 us (12%)
  matrix products  30.1 us (11%)
  local copies, waits for them, and re-layouts  22.3 us (8%)
  between operations  20.4 us (7%)
  other arithmetic  12.9 us (5%)
  starting transfers between devices  12.2 us (4%)
    all_gather x1, waiting for transfers between devices, per_device(): lax.all_gather(slice_part(qkv_weight[0], position, across), ('wrow', 'wco...  63.5 us
    ppermute x12, waiting for transfers between devices, passed_along(): lax.ppermute(shard, axis, [(i, (i + by) % devices) for i in range(devices)])  52.9 us
    all_gather x1, blocking collectives, per_device(): lax.all_gather(slice_part(mod_part, position, across), ('wrow', 'wcol'),...  34.5 us
    ppermute x2, waiting for transfers between devices, from_behind(): return lax.ppermute(shard, axis, pairs)  30.1 us
    dot_general x6, matrix products, project(): jnp.dot(region.reshape(tile_rows * tile_cols, feature_width), matrix, pre...  20.5 us
    ppermute x2, starting transfers between devices, from_behind(): return lax.ppermute(shard, axis, pairs)  7.86 us
    transpose x2, local copies, waits for them, and re-layouts, regroup(): return matrix.reshape(leading, across, along, piece_width).transpose(0, 2...  6.89 us
    select_n x3, other arithmetic, per_device(): results = jnp.where(active, updated, results)  6.86 us
  transfers between devices with their start and end apart: 16, of which 14 were waited for; matrix products, arithmetic and copies ran while one was open for 5% of the time, Pallas kernels for 0%

commit v1 on v0

--- a/solution.py
+++ b/solution.py
@@ -10,6 +10,18 @@
 WIN = 8
 MB = 2
 epsilon = 1e-06
+
+
+def gather_by_bits(shard, axis, dim):
+    ways, here = (lax.axis_size(axis), lax.axis_index(axis))
+    grown, reach = (shard, 1)
+    while reach < ways:
+        theirs = lax.ppermute(grown, axis, [(d, d ^ reach) for d in range(ways)])
+        mine_first = jnp.concatenate([grown, theirs], axis=dim)
+        theirs_first = jnp.concatenate([theirs, grown], axis=dim)
+        grown = jnp.where(here & reach == 0, mine_first, theirs_first)
+        reach = 2 * reach
+    return grown
 
 
 def passed_along(shard, axis, by):
@@ -131,9 +143,7 @@
     along = lax.axis_size("wcol")
     position = lax.axis_index("wrow")
     gathered = (
-        lax.all_gather(
-            slice_part(qkv_weight[0], position, across), ("wrow", "wcol"), axis=1, tiled=True
-        ),
+        gather_by_bits(slice_part(qkv_weight[0], position, across), ("wrow", "wcol"), 1),
         lax.all_gather(
             slice_part(out_weight[0], position, across), ("wrow", "wcol"), axis=1, tiled=True
         ),

time: 280 us -> 330 us (1.18)
  waiting for transfers between devices: 147 us -> 179 us
  other arithmetic: 12.9 us -> 24.7 us
  starting transfers between devices: 12.2 us -> 21.5 us
    all_gather x1 -> x0, waiting for transfers between devices: 63.5 us -> none  [per_device(): lax.all_gather(slice_part(qkv_weight[0], position, across), ('wrow', 'wco...]
    ppermute x0 -> x4, waiting for transfers between devices: none -> 49.9 us  [gather_by_bits(): theirs = lax.ppermute(grown, axis, [(d, d ^ reach) for d in range(ways)])]
    ppermute x12, waiting for transfers between devices: 52.9 us -> 98.7 us  [passed_along(): lax.ppermute(shard, axis, [(i, (i + by) % devices) for i in range(devices)])]
    select_n x0 -> x4, other arithmetic: none -> 8.76 us  [gather_by_bits(): grown = jnp.where(here & reach == 0, mine_first, theirs_first)]
    ppermute x0 -> x4, starting transfers between devices: none -> 7.41 us  [gather_by_bits(): theirs = lax.ppermute(grown, axis, [(d, d ^ reach) for d in range(ways)])]
    transpose x0 -> x1, other arithmetic: none -> 4.14 us  [regroup(): return matrix.reshape(leading, across, along, piece_width).transpose(0, 2...]
  transfers between devices with their start and end apart: 16 -> 19, of which waited for: 14 -> 16; matrix products, arithmetic and copies ran while one was open for 5% -> 8% of each run, Pallas kernels for 0% -> 0%
where the time goes in v1:
time: 330 us; the launch traced here: 329 us
  waiting for transfers between devices  179 us (54%)
  blocking collectives  32.1 us (10%)
  matrix products  31 us (9%)
  other arithmetic  24.7 us (7%)
  starting transfers between devices  21.5 us (7%)
  between operations  20.7 us (6%)
  local copies, waits for them, and re-layouts  19.9 us (6%)
    ppermute x12, waiting for transfers between devices, passed_along(): lax.ppermute(shard, axis, [(i, (i + by) % devices) for i in range(devices)])  98.7 us
    ppermute x4, waiting for transfers between devices, gather_by_bits(): theirs = lax.ppermute(grown, axis, [(d, d ^ reach) for d in range(ways)])  49.9 us
    all_gather x1, blocking collectives, per_device(): lax.all_gather(slice_part(mod_part, position, across), ('wrow', 'wcol'),...  32.1 us
    ppermute x2, waiting for transfers between devices, from_behind(): return lax.ppermute(shard, axis, pairs)  30.2 us
    dot_general x6, matrix products, project(): jnp.dot(region.reshape(tile_rows * tile_cols, feature_width), matrix, pre...  23.5 us
    select_n x4, other arithmetic, gather_by_bits(): grown = jnp.where(here & reach == 0, mine_first, theirs_first)  8.76 us
    ppermute x2, starting transfers between devices, from_behind(): return lax.ppermute(shard, axis, pairs)  7.94 us
    ppermute x4, starting transfers between devices, gather_by_bits(): theirs = lax.ppermute(grown, axis, [(d, d ^ reach) for d in range(ways)])  7.41 us
  transfers between devices with their start and end apart: 19, of which 16 were waited for; matrix products, arithmetic and copies ran while one was open for 8% of the time, Pallas kernels for 0%

profile of v1, /device:TPU:0, one launch (start us, length us, event | category | flops | bytes accessed | tf_op | source)
XLA Modules:
  0.0 328.7 jit_solution(13306286632382749068)
XLA Ops:
  6.5 1.5 copy-done
  8.0 3.1 collective-permute-start.2
  11.2 10.2 %collective-permute-done.2 = bf16[1536,144]{0,1:T(8,128)(2,1)S(1)} collective-permute-done((bf16[1536,144]{0,1:T(8,128)(2,1)S(1)}, bf16[1536,144]{0,1:T(8,128)(2,1)S(1)}, u32[]{:S(2)}, u32[]{:S(2)}) %collective-permute-start.2) | collective-permute-done | bytes 442400 | tf_op jit(solution)/shard_map/ppermute | solution.py:19
  21.5 2.8 collective-permute-start.3
  24.4 37.9 %collective-permute-done.3 = bf16[1536,288]{0,1:T(8,128)(2,1)S(1)} collective-permute-done((bf16[1536,288]{0,1:T(8,128)(2,1)S(1)}, bf16[1536,288]{0,1:T(8,128)(2,1)S(1)}, u32[]{:S(2)}, u32[]{:S(2)}) %collective-permute-start.3) | collective-permute-done | bytes 884768 | tf_op jit(solution)/shard_map/ppermute | solution.py:19
  63.0 1.1 constant_dynamic-slice_fusion
  65.0 1.8 collective-permute-done.4
  66.8 3.8 %maximum_select_fusion.2 = bf16[1536,1152]{0,1:T(8,128)(2,1)} fusion(bf16[1536,576]{0,1:T(8,128)(2,1)} %collective-permute-done.4, bf16[1536,576]{0,1:T(8,128)(2,1)S(1)} %maximum_select_fusion.3, pred[]{:T(512)S(6)} %eq.19), kind=kLoop, calls=%fused_computation.6 | loop fusion | flops 15925248 | bytes 7077889 | tf_op jit(solution)/shard_map/jit(_where)/select_n | solution.py:22
  70.7 1.4 collective-permute-start.5
  72.2 1.3 fusion.47
  73.6 32.1 %all-gather.1 = bf16[16,288,2]{1,2,0:T(2,128)(2,1)S(1)} all-gather(bf16[1,288,2]{1,2,0:T(2,128)(2,1)S(1)} %fusion.63), channel_id=1, replica_groups=mesh['section'=2,'wrow'=4,'wcol'=4] {'wrow','wcol'}, dimensions={0}, use_global_device_ids=true | all-gather | bytes 19584 | tf_op jit(solution)/shard_map/all_gather | solution.py:150
  107.8 0.9 copy-done.9
  113.4 45.2 %collective-permute-done = bf16[4,16,1536]{2,1,0:T(8,128)(2,1)S(1)} collective-permute-done((bf16[4,16,1536]{2,1,0:T(8,128)(2,1)S(1)}, bf16[4,16,1536]{2,1,0:T(8,128)(2,1)S(1)}, u32[]{:S(2)}, u32[]{:S(2)}) %collective-permute-start) | collective-permute-done | bytes 196640 | tf_op jit(solution)/shard_map/ppermute | solution.py:29
  158.5 1.3 fusion.32
  159.8 3.5 %collective-permute-start.1 = (bf16[16,4,1536]{2,1,0:T(4,128)(2,1)S(1)}, bf16[16,4,1536]{2,1,0:T(4,128)(2,1)S(1)}, u32[]{:S(2)}, u32[]{:S(2)}) collective-permute-start(bf16[16,4,1536]{2,1,0:T(4,128)(2,1)S(1)} %slice.177), channel_id=1, source_target_pairs={{0,3},{1,0},{2,1},{3,2},{4,7},{5,4},{6,5},{7,6},{8,11},{9,8},{10,9... | collective-permute-start | bytes 589832 | tf_op jit(solution)/shard_map/ppermute | solution.py:29
  163.4 4.1 %maximum_select_fusion.1 = bf16[1536,2,4,144]{0,3,2,1:T(8,128)(2,1)} fusion(bf16[1536,1,4,144]{0,3,2,1:T(8,128)(2,1)} %bitcast.10, bf16[1536,1,4,144]{0,3,2,1:T(8,128)(2,1)S(1)} %bitcast.131, pred[]{:T(512)S(6)} %eq.19), kind=kLoop, calls=%fused_computation.5 | loop fusion | flops 5308416 | bytes 7077889 | tf_op jit(solution)/shard_map/jit(_where)/select_n | solution.py:22
  167.4 3.4 %copy.61 = bf16[768,4,4,96]{0,3,2,1:T(8,128)(2,1)} copy(bf16[768,4,4,96]{0,3,1,2:T(8,128)(2,1)} %bitcast.139) | data formatting | bytes 4718592 | tf_op jit(solution)/shard_map/transpose | solution.py:132
  170.8 4.1 %fusion = bf16[1536,4,4,144]{0,3,1,2:T(8,128)(2,1)S(1)} fusion(bf16[1536,2,4,144]{0,3,2,1:T(8,128)(2,1)} %bitcast.11, bf16[1536,2,4,144]{0,3,2,1:T(8,128)(2,1)S(1)} %copy-done.2, pred[]{:T(512)S(6)} %eq.18), kind=kLoop, calls=%fused_computation.1 | loop fusion | flops 10616832 | bytes 14155777 | tf_op jit(solution)/shard_map/transpose | solution.py:132
  175.0 3.5 %copy.53 = bf16[1536,4,4,144]{0,3,2,1:T(8,128)(2,1)} copy(bf16[1536,4,4,144]{0,3,1,2:T(8,128)(2,1)S(1)} %fusion) | data formatting | bytes 14155776 | tf_op jit(solution)/shard_map/transpose | solution.py:132
  178.5 5.4 %convolution_convert_fusion.2 = bf16[16,16,2304]{2,1,0:T(8,128)(2,1)S(1)} fusion(bf16[1536,2304,1]{0,1,2:T(8,128)(2,1)} %bitcast.133, s32[]{:T(128)S(6)} %select_n.137, bf16[16,16,1536]{2,1,0:T(8,128)(2,1)S(1)} %fusion.32, bf16[16,4,1536]{2,1,0:T(4,128)(2,1)S(1)} %collective-permute-done.1), kind=kOutput, calls=%fused_computation.4 | convolution fusion | flops 1814102016 | bytes 9240580 | tf_op jit(solution)/shard_map/dot_general | solution.py:74
  185.0 2.5 convolution_convert_fusion.5
  189.4 3.3 %collective-permute-done.6 = bf16[4,16,1536]{2,1,0:T(8,128)(2,1)S(1)} collective-permute-done((bf16[4,16,1536]{2,1,0:T(8,128)(2,1)S(1)}, bf16[4,16,1536]{2,1,0:T(8,128)(2,1)S(1)}, u32[]{:S(2)}, u32[]{:S(2)}) %collective-permute-start.6) | collective-permute-done | bytes 196640 | tf_op jit(solution)/shard_map/ppermute | solution.py:29
  192.8 0.9 copy-done.10
  195.3 6.1 %collective-permute-done.7 = bf16[16,4,1536]{2,1,0:T(4,128)(2,1)S(1)} collective-permute-done((bf16[16,4,1536]{2,1,0:T(4,128)(2,1)S(1)}, bf16[16,4,1536]{2,1,0:T(4,128)(2,1)S(1)}, u32[]{:S(2)}, u32[]{:S(2)}) %collective-permute-start.7) | collective-permute-done | bytes 196640 | tf_op jit(solution)/shard_map/ppermute | solution.py:29
  202.3 3.5 %collective-permute-start.8 = (bf16[16,16,1536]{2,1,0:T(8,128)(2,1)S(1)}, bf16[16,16,1536]{2,1,0:T(8,128)(2,1)S(1)}, u32[]{:S(2)}, u32[]{:S(2)}) collective-permute-start(bf16[16,16,1536]{2,1,0:T(8,128)(2,1)S(1)} %get-tuple-element.21), channel_id=1, source_target_pairs={{0,16},{1,17},{2,18},{3,19},{4,20},{5,21},{6,22},{7,23},{8,24},{9,... | collective-permute-start | bytes 2359304 | tf_op jit(solution)/shard_map/ppermute | solution.py:35
  205.9 13.8 %collective-permute-done.8 = bf16[16,16,1536]{2,1,0:T(8,128)(2,1)S(1)} collective-permute-done((bf16[16,16,1536]{2,1,0:T(8,128)(2,1)S(1)}, bf16[16,16,1536]{2,1,0:T(8,128)(2,1)S(1)}, u32[]{:S(2)}, u32[]{:S(2)}) %collective-permute-start.8) | collective-permute-done | bytes 786464 | tf_op jit(solution)/shard_map/ppermute | solution.py:35
  220.9 3.2 collective-permute-done.9
  224.6 6.3 %collective-permute-done.10 = bf16[16,4,1536]{2,1,0:T(4,128)(2,1)S(1)} collective-permute-done((bf16[16,4,1536]{2,1,0:T(4,128)(2,1)S(1)}, bf16[16,4,1536]{2,1,0:T(4,128)(2,1)S(1)}, u32[]{:S(2)}, u32[]{:S(2)}) %collective-permute-start.10) | collective-permute-done | bytes 196640 | tf_op jit(solution)/shard_map/ppermute | solution.py:29
  230.9 5.4 %convolution_convert_fusion.1 = bf16[16,16,2304]{2,1,0:T(8,128)(2,1)S(1)} fusion(bf16[1536,2304,1]{0,1,2:T(8,128)(2,1)} %bitcast.134, s32[]{:T(128)S(6)} %select_n.137, bf16[16,16,1536]{2,1,0:T(8,128)(2,1)S(1)} %fusion.30, bf16[16,4,1536]{2,1,0:T(4,128)(2,1)S(1)} %collective-permute-done.10), kind=kOutput, calls=%fused_computation.3 | convolution fusion | flops 1814102016 | bytes 9240580 | tf_op jit(solution)/shard_map/dot_general | solution.py:74
  237.5 1.2 fusion.25
  238.7 2.7 convolution_convert_fusion.7
  241.3 1.1 copy.68
  242.4 2.5 convolution_convert_fusion.4
  244.9 1.3 collective-permute-start.11
  246.2 3.9 %collective-permute-done.11 = bf16[4,16,1536]{2,1,0:T(8,128)(2,1)S(1)} collective-permute-done((bf16[4,16,1536]{2,1,0:T(8,128)(2,1)S(1)}, bf16[4,16,1536]{2,1,0:T(8,128)(2,1)S(1)}, u32[]{:S(2)}, u32[]{:S(2)}) %collective-permute-start.11) | collective-permute-done | bytes 196640 | tf_op jit(solution)/shard_map/ppermute | solution.py:29
  251.2 9.0 %collective-permute-done.12 = bf16[16,4,1536]{2,1,0:T(4,128)(2,1)S(1)} collective-permute-done((bf16[16,4,1536]{2,1,0:T(4,128)(2,1)S(1)}, bf16[16,4,1536]{2,1,0:T(4,128)(2,1)S(1)}, u32[]{:S(2)}, u32[]{:S(2)}) %collective-permute-start.12) | collective-permute-done | bytes 196640 | tf_op jit(solution)/shard_map/ppermute | solution.py:29
  260.2 2.2 fusion.46
  262.4 4.4 %collective-permute-start.13 = (bf16[16,16,1536]{2,1,0:T(8,128)(2,1)S(1)}, bf16[16,16,1536]{2,1,0:T(8,128)(2,1)S(1)}, u32[]{:S(2)}, u32[]{:S(2)}) collective-permute-start(bf16[16,16,1536]{2,1,0:T(8,128)(2,1)S(1)} %get-tuple-element.17), channel_id=1, source_target_pairs={{0,16},{1,17},{2,18},{3,19},{4,20},{5,21},{6,22},{7,23},{8,24},{9,... | collective-permute-start | bytes 2359304 | tf_op jit(solution)/shard_map/ppermute | solution.py:35
  266.9 16.4 %collective-permute-done.13 = bf16[16,16,1536]{2,1,0:T(8,128)(2,1)S(1)} collective-permute-done((bf16[16,16,1536]{2,1,0:T(8,128)(2,1)S(1)}, bf16[16,16,1536]{2,1,0:T(8,128)(2,1)S(1)}, u32[]{:S(2)}, u32[]{:S(2)}) %collective-permute-start.13) | collective-permute-done | bytes 786464 | tf_op jit(solution)/shard_map/ppermute | solution.py:35
  284.4 3.2 collective-permute-done.14
  288.0 7.3 %collective-permute-done.15 = bf16[16,4,1536]{2,1,0:T(4,128)(2,1)S(1)} collective-permute-done((bf16[16,4,1536]{2,1,0:T(4,128)(2,1)S(1)}, bf16[16,4,1536]{2,1,0:T(4,128)(2,1)S(1)}, u32[]{:S(2)}, u32[]{:S(2)}) %collective-permute-start.15) | collective-permute-done | bytes 196640 | tf_op jit(solution)/shard_map/ppermute | solution.py:29
  295.3 5.4 %convolution_convert_fusion = bf16[16,16,2304]{2,1,0:T(8,128)(2,1)S(1)} fusion(bf16[1536,2304,1]{0,1,2:T(8,128)(2,1)} %bitcast.135, s32[]{:T(128)S(6)} %select_n.137, bf16[16,16,1536]{2,1,0:T(8,128)(2,1)S(1)} %fusion.28, bf16[16,4,1536]{2,1,0:T(4,128)(2,1)S(1)} %collective-permute-done.15), kind=kOutput, calls=%fused_computation.2 | convolution fusion | flops 1814102016 | bytes 9240580 | tf_op jit(solution)/shard_map/dot_general | solution.py:74
  302.2 1.3 convolution_convert_fusion.6
  303.6 2.5 convolution_convert_fusion.3
  306.2 5.1 %collective-permute-done.16 = bf16[4,16,1536]{2,1,0:T(8,128)(2,1)S(1)} collective-permute-done((bf16[4,16,1536]{2,1,0:T(8,128)(2,1)S(1)}, bf16[4,16,1536]{2,1,0:T(8,128)(2,1)S(1)}, u32[]{:S(2)}, u32[]{:S(2)}) %collective-permute-start.16) | collective-permute-done | bytes 196640 | tf_op jit(solution)/shard_map/ppermute | solution.py:29
  311.6 1.1 copy.97
  312.8 6.2 %collective-permute-done.17 = bf16[16,4,1536]{2,1,0:T(4,128)(2,1)S(1)} collective-permute-done((bf16[16,4,1536]{2,1,0:T(4,128)(2,1)S(1)}, bf16[16,4,1536]{2,1,0:T(4,128)(2,1)S(1)}, u32[]{:S(2)}, u32[]{:S(2)}) %collective-permute-start.17) | collective-permute-done | bytes 196640 | tf_op jit(solution)/shard_map/ppermute | solution.py:29
  319.0 2.8 fusion.45
  (114 shorter events, 15.2 us)
Async XLA Ops:
  6.5 1.5 copy-start
  6.5 160.9 %all-gather.4.cloned.1.call-start = ((), (), s32[]{:S(2)}) async-start(), calls=%async_computation | async-start | bytes 2506752 | tf_op jit(solution)/shard_map/all_gather | solution.py:147
  8.0 13.3 %collective-permute-start.2 = (bf16[1536,144]{0,1:T(8,128)(2,1)S(1)}, bf16[1536,144]{0,1:T(8,128)(2,1)S(1)}, u32[]{:S(2)}, u32[]{:S(2)}) collective-permute-start(bf16[1536,144]{0,1:T(8,128)(2,1)S(1)} %dynamic-slice_bitcast_fusion), channel_id=1, source_target_pairs={{0,1},{1,0},{2,3},{3,2},{4,5},{5,4},{6,7},{7,6},{8,9},{9,8},{10,11... | collective-permute-start | bytes 1327112 | tf_op jit(solution)/shard_map/ppermute | solution.py:19
  21.5 40.7 %collective-permute-start.3 = (bf16[1536,288]{0,1:T(8,128)(2,1)S(1)}, bf16[1536,288]{0,1:T(8,128)(2,1)S(1)}, u32[]{:S(2)}, u32[]{:S(2)}) collective-permute-start(bf16[1536,288]{0,1:T(8,128)(2,1)S(1)} %maximum_select_fusion.4), channel_id=1, source_target_pairs={{0,2},{1,3},{2,0},{3,1},{4,6},{5,7},{6,4},{7,5},{8,10},{9,11},{10,... | collective-permute-start | bytes 2654216 | tf_op jit(solution)/shard_map/ppermute | solution.py:19
  63.0 3.9 %collective-permute-start.4 = (bf16[1536,576]{0,1:T(8,128)(2,1)S(1)}, bf16[1536,576]{0,1:T(8,128)(2,1)}, u32[]{:S(2)}, u32[]{:S(2)}) collective-permute-start(bf16[1536,576]{0,1:T(8,128)(2,1)S(1)} %maximum_select_fusion.3), channel_id=1, source_target_pairs={{0,4},{1,5},{2,6},{3,7},{4,0},{5,1},{6,2},{7,3},{8,12},{9,13},{10,... | collective-permute-start | bytes 5308424 | tf_op jit(solution)/shard_map/ppermute | solution.py:19
  65.0 7.1 %copy-start.15 = (s32[2]{0:T(128)S(1)}, s32[2]{0:T(128)}, u32[]{:S(2)}) copy-start(s32[2]{0:T(128)} %param.7) | copy-start | bytes 28
  66.8 39.9 %copy-start.3 = (bf16[2,16,16,1536]{3,2,1,0:T(8,128)(2,1)S(1)}, bf16[2,16,16,1536]{3,2,1,0:T(8,128)(2,1)}, u32[]{:S(2)}) copy-start(bf16[2,16,16,1536]{3,2,1,0:T(8,128)(2,1)} %param.6) | copy-start | bytes 4718596
  70.7 100.2 %collective-permute-start.5 = (bf16[1536,1152]{0,1:T(8,128)(2,1)}, bf16[1536,1152]{0,1:T(8,128)(2,1)}, u32[]{:S(2)}, u32[]{:S(2)}) collective-permute-start(bf16[1536,1152]{0,1:T(8,128)(2,1)} %maximum_select_fusion.2), channel_id=1, source_target_pairs={{0,8},{1,9},{2,10},{3,11},{4,12},{5,13},{6,14},{7,15},{8,0},{9,1},... | collective-permute-start | bytes 10616840 | tf_op jit(solution)/shard_map/ppermute | solution.py:19
  107.0 1.7 copy-start.14
  107.8 0.9 copy-start.9
  108.7 49.8 %collective-permute-start = (bf16[4,16,1536]{2,1,0:T(8,128)(2,1)S(1)}, bf16[4,16,1536]{2,1,0:T(8,128)(2,1)S(1)}, u32[]{:S(2)}, u32[]{:S(2)}) collective-permute-start(bf16[4,16,1536]{2,1,0:T(8,128)(2,1)S(1)} %slice.176), channel_id=1, source_target_pairs={{0,12},{4,0},{8,4},{12,8},{1,13},{5,1},{9,5},{13,9},{2,14},{6,2},{... | collective-permute-start | bytes 589832 | tf_op jit(solution)/shard_map/ppermute | solution.py:29
  159.8 18.7 %collective-permute-start.1 = (bf16[16,4,1536]{2,1,0:T(4,128)(2,1)S(1)}, bf16[16,4,1536]{2,1,0:T(4,128)(2,1)S(1)}, u32[]{:S(2)}, u32[]{:S(2)}) collective-permute-start(bf16[16,4,1536]{2,1,0:T(4,128)(2,1)S(1)} %slice.177), channel_id=1, source_target_pairs={{0,3},{1,0},{2,1},{3,2},{4,7},{5,4},{6,5},{7,6},{8,11},{9,8},{10,9... | collective-permute-start | bytes 589832 | tf_op jit(solution)/shard_map/ppermute | solution.py:29
  167.4 3.4 %copy-start.2 = (bf16[1536,2,4,144]{0,3,2,1:T(8,128)(2,1)S(1)}, bf16[1536,2,4,144]{0,3,2,1:T(8,128)(2,1)}, u32[]{:S(2)}) copy-start(bf16[1536,2,4,144]{0,3,2,1:T(8,128)(2,1)} %maximum_select_fusion.1) | copy-start | bytes 10616836
  187.5 5.1 %collective-permute-start.6 = (bf16[4,16,1536]{2,1,0:T(8,128)(2,1)S(1)}, bf16[4,16,1536]{2,1,0:T(8,128)(2,1)S(1)}, u32[]{:S(2)}, u32[]{:S(2)}) collective-permute-start(bf16[4,16,1536]{2,1,0:T(8,128)(2,1)S(1)} %slice.181), channel_id=1, source_target_pairs={{0,4},{4,8},{8,12},{12,0},{1,5},{5,9},{9,13},{13,1},{2,6},{6,10},{... | collective-permute-start | bytes 589832 | tf_op jit(solution)/shard_map/ppermute | solution.py:29
  189.4 12.1 %copy-start.4 = (bf16[2,16,16,1536]{3,2,1,0:T(8,128)(2,1)S(1)}, bf16[2,16,16,1536]{3,2,1,0:T(8,128)(2,1)}, u32[]{:S(2)}) copy-start(bf16[2,16,16,1536]{3,2,1,0:T(8,128)(2,1)} %param.6) | copy-start | bytes 4718596
  192.8 0.9 copy-start.10
  193.8 7.5 %collective-permute-start.7 = (bf16[16,4,1536]{2,1,0:T(4,128)(2,1)S(1)}, bf16[16,4,1536]{2,1,0:T(4,128)(2,1)S(1)}, u32[]{:S(2)}, u32[]{:S(2)}) collective-permute-start(bf16[16,4,1536]{2,1,0:T(4,128)(2,1)S(1)} %slice.182), channel_id=1, source_target_pairs={{0,1},{1,2},{2,3},{3,0},{4,5},{5,6},{6,7},{7,4},{8,9},{9,10},{10,1... | collective-permute-start | bytes 589832 | tf_op jit(solution)/shard_map/ppermute | solution.py:29
  195.3 6.3 %copy-start.11 = (bf16[16,16,1536]{2,1,0:T(8,128)(2,1)S(1)}, bf16[16,16,1536]{2,1,0:T(8,128)(2,1)}, u32[]{:S(2)}) copy-start(bf16[16,16,1536]{2,1,0:T(8,128)(2,1)} %copy-done.10) | copy-start | bytes 2359300
  202.3 17.4 %collective-permute-start.8 = (bf16[16,16,1536]{2,1,0:T(8,128)(2,1)S(1)}, bf16[16,16,1536]{2,1,0:T(8,128)(2,1)S(1)}, u32[]{:S(2)}, u32[]{:S(2)}) collective-permute-start(bf16[16,16,1536]{2,1,0:T(8,128)(2,1)S(1)} %get-tuple-element.21), channel_id=1, source_target_pairs={{0,16},{1,17},{2,18},{3,19},{4,20},{5,21},{6,22},{7,23},{8,24},{9,... | collective-permute-start | bytes 2359304 | tf_op jit(solution)/shard_map/ppermute | solution.py:35
  220.0 4.3 %copy-start.5 = (bf16[16,16,1536]{2,1,0:T(8,128)(2,1)}, bf16[16,16,1536]{2,1,0:T(8,128)(2,1)S(1)}, u32[]{:S(2)}) copy-start(bf16[16,16,1536]{2,1,0:T(8,128)(2,1)S(1)} %get-tuple-element.19) | copy-start | bytes 2359300
  220.8 3.2 collective-permute-start.9
  224.3 6.6 %collective-permute-start.10 = (bf16[16,4,1536]{2,1,0:T(4,128)(2,1)S(1)}, bf16[16,4,1536]{2,1,0:T(4,128)(2,1)S(1)}, u32[]{:S(2)}, u32[]{:S(2)}) collective-permute-start(bf16[16,4,1536]{2,1,0:T(4,128)(2,1)S(1)} %slice.187), channel_id=1, source_target_pairs={{0,3},{1,0},{2,1},{3,2},{4,7},{5,4},{6,5},{7,6},{8,11},{9,8},{10,9... | collective-permute-start | bytes 589832 | tf_op jit(solution)/shard_map/ppermute | solution.py:29
  244.9 5.1 %collective-permute-start.11 = (bf16[4,16,1536]{2,1,0:T(8,128)(2,1)S(1)}, bf16[4,16,1536]{2,1,0:T(8,128)(2,1)S(1)}, u32[]{:S(2)}, u32[]{:S(2)}) collective-permute-start(bf16[4,16,1536]{2,1,0:T(8,128)(2,1)S(1)} %slice.191), channel_id=1, source_target_pairs={{0,4},{4,8},{8,12},{12,0},{1,5},{5,9},{9,13},{13,1},{2,6},{6,10},{... | collective-permute-start | bytes 589832 | tf_op jit(solution)/shard_map/ppermute | solution.py:29
  250.2 0.9 copy-start.8
  251.2 9.0 %collective-permute-start.12 = (bf16[16,4,1536]{2,1,0:T(4,128)(2,1)S(1)}, bf16[16,4,1536]{2,1,0:T(4,128)(2,1)S(1)}, u32[]{:S(2)}, u32[]{:S(2)}) collective-permute-start(bf16[16,4,1536]{2,1,0:T(4,128)(2,1)S(1)} %slice.192), channel_id=1, source_target_pairs={{0,1},{1,2},{2,3},{3,0},{4,5},{5,6},{6,7},{7,4},{8,9},{9,10},{10,1... | collective-permute-start | bytes 589832 | tf_op jit(solution)/shard_map/ppermute | solution.py:29
  260.2 6.7 %copy-start.13 = (f32[1,4608]{1,0:T(1,128)S(1)}, f32[1,4608]{1,0:T(1,128)}, u32[]{:S(2)}) copy-start(f32[1,4608]{1,0:T(1,128)} %get-tuple-element.31) | copy-start | bytes 55300
  262.4 20.9 %collective-permute-start.13 = (bf16[16,16,1536]{2,1,0:T(8,128)(2,1)S(1)}, bf16[16,16,1536]{2,1,0:T(8,128)(2,1)S(1)}, u32[]{:S(2)}, u32[]{:S(2)}) collective-permute-start(bf16[16,16,1536]{2,1,0:T(8,128)(2,1)S(1)} %get-tuple-element.17), channel_id=1, source_target_pairs={{0,16},{1,17},{2,18},{3,19},{4,20},{5,21},{6,22},{7,23},{8,24},{9,... | collective-permute-start | bytes 2359304 | tf_op jit(solution)/shard_map/ppermute | solution.py:35
  283.6 4.3 %copy-start.6 = (bf16[16,16,1536]{2,1,0:T(8,128)(2,1)}, bf16[16,16,1536]{2,1,0:T(8,128)(2,1)S(1)}, u32[]{:S(2)}) copy-start(bf16[16,16,1536]{2,1,0:T(8,128)(2,1)S(1)} %get-tuple-element.15) | copy-start | bytes 2359300
  284.4 3.2 collective-permute-start.14
  287.9 7.4 %collective-permute-start.15 = (bf16[16,4,1536]{2,1,0:T(4,128)(2,1)S(1)}, bf16[16,4,1536]{2,1,0:T(4,128)(2,1)S(1)}, u32[]{:S(2)}, u32[]{:S(2)}) collective-permute-start(bf16[16,4,1536]{2,1,0:T(4,128)(2,1)S(1)} %slice.197), channel_id=1, source_target_pairs={{0,3},{1,0},{2,1},{3,2},{4,7},{5,4},{6,5},{7,6},{8,11},{9,8},{10,9... | collective-permute-start | bytes 589832 | tf_op jit(solution)/shard_map/ppermute | solution.py:29
  306.1 5.1 %collective-permute-start.16 = (bf16[4,16,1536]{2,1,0:T(8,128)(2,1)S(1)}, bf16[4,16,1536]{2,1,0:T(8,128)(2,1)S(1)}, u32[]{:S(2)}, u32[]{:S(2)}) collective-permute-start(bf16[4,16,1536]{2,1,0:T(8,128)(2,1)S(1)} %slice.201), channel_id=1, source_target_pairs={{0,4},{4,8},{8,12},{12,0},{1,5},{5,9},{9,13},{13,1},{2,6},{6,10},{... | collective-permute-start | bytes 589832 | tf_op jit(solution)/shard_map/ppermute | solution.py:29
  311.4 1.4 copy-start.12
  311.5 7.5 %collective-permute-start.17 = (bf16[16,4,1536]{2,1,0:T(4,128)(2,1)S(1)}, bf16[16,4,1536]{2,1,0:T(4,128)(2,1)S(1)}, u32[]{:S(2)}, u32[]{:S(2)}) collective-permute-start(bf16[16,4,1536]{2,1,0:T(4,128)(2,1)S(1)} %slice.202), channel_id=1, source_target_pairs={{0,1},{1,2},{2,3},{3,0},{4,5},{5,6},{6,7},{7,4},{8,9},{9,10},{10,1... | collective-permute-start | bytes 589832 | tf_op jit(solution)/shard_map/ppermute | solution.py:29
  311.6 7.5 %copy-start.7 = (bf16[16,16,1536]{2,1,0:T(8,128)(2,1)S(1)}, bf16[16,16,1536]{2,1,0:T(8,128)(2,1)}, u32[]{:S(2)}) copy-start(bf16[16,16,1536]{2,1,0:T(8,128)(2,1)} %copy-done.6) | copy-start | bytes 2359300
  319.0 2.9 copy-start.1
Sparse Core Ops, SparseCore 0:
  65.1 49.8 all-gather.3
